TPU v7x, 256 devices: a whole 4x4x8 slice. The times are simulated.
256 devices in a mesh: dom: 8 (over y, x_lo), sub: 32 (over z, x_hi, core).
Axes of the slice: x: 4 (x_hi: 2, x_lo: 2; x = x_hi * 2 + x_lo), y: 4, z: 8, core: 2. Of those that a mesh axis runs over, the one named last changes fastest.
Arguments:
- fine_residual: float32 [3, 1048576], P(None, ('dom', 'sub')), may hold values from -6 to 6
- bonds: bfloat16 [32, 3, 3, 1048576], P(None, None, None, ('dom', 'sub')), may hold values from -0.3125 to 0.3125
- bond_col: int32 [32, 1048576], P(None, ('dom', 'sub')), may hold values from 0 to 5119, as said below
- ghost_points: int32 [256, 2, 512], P(('dom', 'sub')), may hold values from -1 to 4095, as said below
- fine_dinv: float32 [3, 3, 1048576], P(None, None, ('dom', 'sub')), may hold values from -0.2 to 1.6
- aggregate: int32 [1048576], P(('dom', 'sub')), may hold values from 0 to 131071, as said below
- coarse_dinv: float32 [3, 3, 131072], P(None, None, 'sub'), may hold values from -0.071 to 0.566
- coarse_couple: float32 [4, 131072], P(None, 'sub'), may hold values from 0.08 to 0.24
Outputs:
- preconditioned: float32 [3, 1048576], P(None, ('dom', 'sub'))
Inputs may be any that keep to these rules, and one draw needn't show every extreme that they name: ghost_points[r, 0, :] lists distinct local points of the previous run of r, ghost_points[r, 1, :] of the next run; each list holds 128 to 512 entries, followed by -1; in every draw some run has both lists full. bond_col[0, i] is i's own local index; a column below 4096 is a local point of the run, 4096 + s names slot s from the previous run and 4608 + s slot s from the next run; only slots that hold a point are named. A point of a run with sub-partition index s lies in an aggregate s * 4096 to (s + 1) * 4096 - 1.
All inputs are finite; a program needn't handle non-finite values.
Results may differ from a plain program's by a relative error of at most 0.0014.
Values may be sent and summed in bfloat16 or wider, within the bound.
No kernel may reach another device: no remote copies, remote signals or barrier semaphores. Data moves between devices by JAX's collectives and lax.ppermute only.
A program may use at most 64 MiB of HBM per device.

v0:
```python
import math
import jax
import jax.numpy as jnp
from jax import lax
from jax.sharding import PartitionSpec as P

SWEEPS = 3
JAC = 6
LOW_EIG = 0.3
HIGH_EIG = 2.2


def with_halo(x, sides, width, wrap):
    for axis, dim in sides:
        peers, length = (lax.axis_size(axis), x.shape[dim])
        up = [(i, (i + 1) % peers) for i in range(peers if wrap else peers - 1)]
        down = [(j, i) for i, j in up]
        last = lax.slice_in_dim(x, length - width, length, axis=dim)
        initial = lax.slice_in_dim(x, 0, width, axis=dim)
        before = lax.ppermute(last, axis, up)
        after = lax.ppermute(initial, axis, down)
        x = jnp.concatenate([before, x, after], axis=dim)
    return x


def passed_along(value, axis, steps):
    count = lax.axis_size(axis)
    pairs = [(source, (source + steps) % count) for source in range(count)]
    return lax.ppermute(value, axis, pairs)


def shortened(x):

    def short(part):
        return part.astype(jnp.bfloat16) if part.dtype == jnp.float32 else part

    return jax.tree.map(short, x)


def point_solve(matrix, vector):
    return jnp.sum(matrix * vector[None, :, :], axis=1)


def lookup(table, indices, precision):
    rows = table.shape[0]
    width = table.shape[1]
    groups = -(-width // 128)
    padded = table.reshape(rows * groups, 128)
    flat = indices.reshape(-1)
    total = flat.shape[0]
    block = math.gcd(total, 8192)
    lanes = jnp.arange(128, dtype=jnp.int32)
    group_ids = jnp.arange(groups, dtype=jnp.int32)

    def lookup_one_block(piece):
        onehot = (piece[None, :] % 128 == lanes[:, None]).astype(table.dtype)
        spread = jnp.dot(
            padded, onehot, preferred_element_type=jnp.float32, precision=precision
        ).reshape(rows, groups, block)
        chosen = piece[None, :] // 128 == group_ids[:, None]
        return jnp.sum(jnp.where(chosen[None, :, :], spread, 0.0), axis=1)

    result = lax.map(lookup_one_block, flat.reshape(total // block, block))
    return result.transpose(1, 0, 2).reshape((rows,) + indices.shape)


def accumulate(values, targets, count):
    points = values.shape[1]
    groups = -(-count // 128)
    block = math.gcd(points, 2048)
    lanes = jnp.arange(128, dtype=jnp.int32)
    group_ids = jnp.arange(groups, dtype=jnp.int32)
    value_blocks = values.reshape(3, points // block, block).transpose(1, 0, 2)
    target_blocks = targets.reshape(points // block, block)

    def accumulate_one_block(total, pieces):
        piece_values, piece_targets = pieces
        onehot = (piece_targets[:, None] % 128 == lanes[None, :]).astype(jnp.float32)
        chosen = piece_targets[None, :] // 128 == group_ids[:, None]
        spread = jnp.where(chosen[None, :, :], piece_values[:, None, :], 0.0).reshape(
            3 * groups, block
        )
        return (
            total
            + jnp.dot(
                spread, onehot, preferred_element_type=jnp.float32, precision=lax.Precision.HIGHEST
            ),
            None,
        )

    start = jnp.zeros((3 * groups, 128), jnp.float32)
    total, unused = lax.scan(accumulate_one_block, start, (value_blocks, target_blocks))
    return total.reshape(3, groups * 128)


def body(
    fine_residual, bonds, bond_col, ghost_points, fine_dinv, aggregate, coarse_dinv, coarse_couple
):
    wanted_lists = with_halo(ghost_points, (("sub", 0),), 1, True)
    for_next = wanted_lists[2, 0]
    for_prev = wanted_lists[0, 1]
    center_eig = (HIGH_EIG + LOW_EIG) / 2.0
    half_range = (HIGH_EIG - LOW_EIG) / 2.0
    factor = half_range / center_eig
    update = point_solve(fine_dinv, fine_residual) / center_eig
    smoothed = update
    for iteration in range(SWEEPS):
        packed = smoothed.astype(jnp.bfloat16)

        def select_points(wanted):
            picked = lookup(packed, jnp.maximum(wanted, 0), None)
            return jnp.where(wanted[None, :] >= 0, picked, 0.0).astype(jnp.bfloat16)

        from_prev = passed_along(select_points(for_next), "sub", 1)
        from_next = passed_along(select_points(for_prev), "sub", -1)
        gathered = lookup(
            jnp.concatenate([packed, from_prev, from_next], axis=1), bond_col, None
        ).astype(jnp.bfloat16)
        remainder = (
            fine_residual
            - smoothed
            - jnp.einsum("kcep,ekp->cp", bonds, gathered, preferred_element_type=jnp.float32)
        )
        factor_new = 1.0 / (2.0 * center_eig / half_range - factor)
        update = factor_new * factor * update + 2.0 * factor_new / half_range * point_solve(
            fine_dinv, remainder
        )
        smoothed = smoothed + update
        factor = factor_new
    per_group = coarse_dinv.shape[2]
    local_agg = aggregate - lax.axis_index("sub") * per_group
    rhs_part = accumulate(fine_residual, local_agg, per_group)
    coarse_rhs = lax.psum(rhs_part, "dom")
    coarse_base = point_solve(coarse_dinv, coarse_rhs)
    coarse = coarse_base
    for iteration in range(JAC - 1):
        layers = with_halo(shortened(coarse[None]), (("sub", 0),), 1, False)
        border = jnp.zeros((3, 1), jnp.float32)
        before = jnp.concatenate([border, coarse[:, :-1]], axis=1)
        after = jnp.concatenate([coarse[:, 1:], border], axis=1)
        below, above, before, after = (layers[0], layers[2], before, after)
        coarse = coarse_base + (
            coarse_couple[0] * below
            + coarse_couple[1] * above
            + coarse_couple[2] * before
            + coarse_couple[3] * after
        )
    return smoothed + lookup(coarse, local_agg, lax.Precision.HIGHEST)


def solution(mesh):
    placed = (
        P(None, ("dom", "sub")),
        P(None, None, None, ("dom", "sub")),
        P(None, ("dom", "sub")),
        P(("dom", "sub"), None, None),
        P(None, None, ("dom", "sub")),
        P(("dom", "sub")),
        P(None, None, "sub"),
        P(None, "sub"),
    )
    return jax.shard_map(
        body, mesh=mesh, in_specs=placed, out_specs=P(None, ("dom", "sub")), check_vma=False
    )
```

profile of v0, /device:TPU:101, one launch (start us, length us, event | category | flops | bytes accessed | tf_op | source)
XLA Modules:
  0.0 297.3 jit_solution(10661571524658893954)
XLA Ops:
  0.7 4.7 %collective-permute-start.2 = (s32[1,2,512]{2,1,0:T(2,128)}, s32[1,2,512]{2,1,0:T(2,128)S(1)}, u32[]{:S(2)}, u32[]{:S(2)}) collective-permute-start(s32[1,2,512]{2,1,0:T(2,128)} %param.19), channel_id=1, source_target_pairs={{0,1},{1,2},{2,3},{3,4},{4,5},{5,6},{6,7},{7,8},{8,9},{9,10},{10,1... | collective-permute-start | bytes 12296 | tf_op jit(solution)/shard_map/ppermute | solution.py:20
  6.7 3.5 %while.39 = (s32[]{:T(128)}, f32[96,128]{1,0:T(8,128)S(1)}, s32[2,2048]{1,0:T(2,128)S(1)}, f32[2,3,2048]{2,1,0:T(4,128)}, s32[]{:T(128)}, /*index=5*/s32[]{:T(128)}) while((s32[]{:T(128)}, f32[96,128]{1,0:T(8,128)S(1)}, s32[2,2048]{1,0:T(2,128)S(1)}, f32[2,3,2048]{2,1,0:T(4,128)}, s32[]{:T(128)}, /*index=5*/s32[]{:T(128)}) %tuple.160), condition=%wide.region_20.21_spmd.clone, body=%wide.region_19.20_spmd.clone.sunk | while | flops 302592000 | bytes 1933399 | solution.py:92
  10.2 27.8 %psum.7 = f32[3,4096]{1,0:T(4,128)S(1)} all-reduce(f32[3,4096]{1,0:T(4,128)S(1)} %reshape.539), channel_id=1, replica_groups=mesh['dom'=8,'sub'=32] {'dom'}, use_global_device_ids=true, to_apply=%region_21.22 | all-reduce | flops 12288 | bytes 98304 | tf_op jit(solution)/shard_map/psum | solution.py:133
  38.7 8.5 %collective-permute-start.8 = (bf16[1,3,4096]{2,1,0:T(4,128)(2,1)}, bf16[1,3,4096]{2,1,0:T(4,128)(2,1)}, u32[]{:S(2)}, u32[]{:S(2)}) collective-permute-start(bf16[1,3,4096]{2,1,0:T(4,128)(2,1)} %convert_bitcast_fusion.7), channel_id=1, source_target_pairs={{0,1},{1,2},{2,3},{3,4},{4,5},{5,6},{6,7},{7,8},{8,9},{9,10},{10,1... | collective-permute-start | bytes 73736 | tf_op jit(solution)/shard_map/ppermute | solution.py:20
  47.2 1.9 collective-permute-start.9
  52.0 5.4 %collective-permute-start.1 = (bf16[3,512]{1,0:T(4,128)(2,1)S(1)}, bf16[3,512]{1,0:T(4,128)(2,1)S(1)}, u32[]{:S(2)}, u32[]{:S(2)}) collective-permute-start(bf16[3,512]{1,0:T(4,128)(2,1)S(1)} %select_convert_fusion.5), channel_id=1, source_target_pairs={{0,1},{1,2},{2,3},{3,4},{4,5},{5,6},{6,7},{7,8},{8,9},{9,10},{10,1... | collective-permute-start | bytes 9224 | tf_op jit(solution)/shard_map/ppermute | solution.py:29
  59.1 5.6 %collective-permute-done.3 = bf16[3,512]{1,0:T(4,128)(2,1)S(1)} collective-permute-done((bf16[3,512]{1,0:T(4,128)(2,1)S(1)}, bf16[3,512]{1,0:T(4,128)(2,1)S(1)}, u32[]{:S(2)}, u32[]{:S(2)}) %collective-permute-start.3) | collective-permute-done | bytes 3104 | tf_op jit(solution)/shard_map/ppermute | solution.py:29
  65.2 43.8 %while.36 = (s32[]{:T(128)}, bf16[16,3,8192]{2,1,0:T(4,128)(2,1)S(1)}, s32[16,8192]{1,0:T(8,128)}, bf16[120,128]{1,0:T(8,128)(2,1)S(1)}, s32[]{:T(128)}) while((s32[]{:T(128)}, bf16[16,3,8192]{2,1,0:T(4,128)(2,1)S(1)}, s32[16,8192]{1,0:T(8,128)}, bf16[120,128]{1,0:T(8,128)(2,1)S(1)}, s32[]{:T(128)}) %tuple.151), condition=%wide.region_5.6_spmd.clone, body=%wide.region_3.5_spmd.clone.sunk | while | flops 255139840 | bytes 8960069 | solution.py:63
  115.6 5.5 %collective-permute-done.5 = bf16[3,512]{1,0:T(4,128)(2,1)S(1)} collective-permute-done((bf16[3,512]{1,0:T(4,128)(2,1)S(1)}, bf16[3,512]{1,0:T(4,128)(2,1)S(1)}, u32[]{:S(2)}, u32[]{:S(2)}) %collective-permute-start.5) | collective-permute-done | bytes 3104 | tf_op jit(solution)/shard_map/ppermute | solution.py:29
  122.2 55.9 %while.37 = (s32[]{:T(128)}, bf16[16,3,8192]{2,1,0:T(4,128)(2,1)S(1)}, s32[16,8192]{1,0:T(8,128)}, bf16[120,128]{1,0:T(8,128)(2,1)}, s32[]{:T(128)}) while((s32[]{:T(128)}, bf16[16,3,8192]{2,1,0:T(4,128)(2,1)S(1)}, s32[16,8192]{1,0:T(8,128)}, bf16[120,128]{1,0:T(8,128)(2,1)}, s32[]{:T(128)}) %tuple.154), condition=%wide.region_11.12_spmd.clone, body=%wide.region_9.11_spmd.clone.sunk | while | flops 255139840 | bytes 8960069 | solution.py:63
  184.5 5.6 %collective-permute-done.7 = bf16[3,512]{1,0:T(4,128)(2,1)S(1)} collective-permute-done((bf16[3,512]{1,0:T(4,128)(2,1)S(1)}, bf16[3,512]{1,0:T(4,128)(2,1)S(1)}, u32[]{:S(2)}, u32[]{:S(2)}) %collective-permute-start.7) | collective-permute-done | bytes 3104 | tf_op jit(solution)/shard_map/ppermute | solution.py:29
  191.2 55.8 %while.38 = (s32[]{:T(128)}, bf16[16,3,8192]{2,1,0:T(4,128)(2,1)S(1)}, s32[16,8192]{1,0:T(8,128)}, bf16[120,128]{1,0:T(8,128)(2,1)}, s32[]{:T(128)}) while((s32[]{:T(128)}, bf16[16,3,8192]{2,1,0:T(4,128)(2,1)S(1)}, s32[16,8192]{1,0:T(8,128)}, bf16[120,128]{1,0:T(8,128)(2,1)}, s32[]{:T(128)}) %tuple.157), condition=%wide.region_17.18_spmd.clone, body=%wide.region_15.17_spmd.clone.sunk | while | flops 255139840 | bytes 8960069 | solution.py:63
  251.9 2.0 collective-permute-start.10
  253.8 2.4 collective-permute-start.11
  256.3 6.4 %collective-permute-done.11 = bf16[1,3,4096]{2,1,0:T(4,128)(2,1)S(1)} collective-permute-done((bf16[1,3,4096]{2,1,0:T(4,128)(2,1)S(1)}, bf16[1,3,4096]{2,1,0:T(4,128)(2,1)S(1)}, u32[]{:S(2)}, u32[]{:S(2)}) %collective-permute-start.11) | collective-permute-done | bytes 24608 | tf_op jit(solution)/shard_map/ppermute | solution.py:21
  262.8 1.9 collective-permute-start.12
  264.7 2.4 collective-permute-start.13
  267.3 6.3 %collective-permute-done.13 = bf16[1,3,4096]{2,1,0:T(4,128)(2,1)S(1)} collective-permute-done((bf16[1,3,4096]{2,1,0:T(4,128)(2,1)S(1)}, bf16[1,3,4096]{2,1,0:T(4,128)(2,1)S(1)}, u32[]{:S(2)}, u32[]{:S(2)}) %collective-permute-start.13) | collective-permute-done | bytes 24608 | tf_op jit(solution)/shard_map/ppermute | solution.py:21
  273.7 1.9 collective-permute-start.14
  275.6 2.4 collective-permute-start.15
  278.1 6.3 %collective-permute-done.15 = bf16[1,3,4096]{2,1,0:T(4,128)(2,1)S(1)} collective-permute-done((bf16[1,3,4096]{2,1,0:T(4,128)(2,1)S(1)}, bf16[1,3,4096]{2,1,0:T(4,128)(2,1)S(1)}, u32[]{:S(2)}, u32[]{:S(2)}) %collective-permute-start.15) | collective-permute-done | bytes 24608 | tf_op jit(solution)/shard_map/ppermute | solution.py:21
  284.6 1.9 collective-permute-start.16
  286.5 2.4 collective-permute-start.17
  289.0 6.3 %collective-permute-done.17 = bf16[1,3,4096]{2,1,0:T(4,128)(2,1)S(1)} collective-permute-done((bf16[1,3,4096]{2,1,0:T(4,128)(2,1)S(1)}, bf16[1,3,4096]{2,1,0:T(4,128)(2,1)S(1)}, u32[]{:S(2)}, u32[]{:S(2)}) %collective-permute-start.17) | collective-permute-done | bytes 24608 | tf_op jit(solution)/shard_map/ppermute | solution.py:21
  (477 shorter events, 186.2 us)
Async XLA Ops:
  0.0 51.6 %collective-permute-start = (s32[1,2,512]{2,1,0:T(2,128)}, s32[1,2,512]{2,1,0:T(2,128)S(1)}, u32[]{:S(2)}, u32[]{:S(2)}) collective-permute-start(s32[1,2,512]{2,1,0:T(2,128)} %param.19), channel_id=1, source_target_pairs={{1,0},{2,1},{3,2},{4,3},{5,4},{6,5},{7,6},{8,7},{9,8},{10,9},{11,1... | collective-permute-start | bytes 12296 | tf_op jit(solution)/shard_map/ppermute | solution.py:21
  0.7 56.7 %collective-permute-start.2 = (s32[1,2,512]{2,1,0:T(2,128)}, s32[1,2,512]{2,1,0:T(2,128)S(1)}, u32[]{:S(2)}, u32[]{:S(2)}) collective-permute-start(s32[1,2,512]{2,1,0:T(2,128)} %param.19), channel_id=1, source_target_pairs={{0,1},{1,2},{2,3},{3,4},{4,5},{5,6},{6,7},{7,8},{8,9},{9,10},{10,1... | collective-permute-start | bytes 12296 | tf_op jit(solution)/shard_map/ppermute | solution.py:20
  6.1 52.0 %copy-start.17 = (s32[32,4096]{1,0:T(8,128)S(1)}, s32[32,4096]{1,0:T(8,128)}, u32[]{:S(2)}) copy-start(s32[32,4096]{1,0:T(8,128)} %param.18) | copy-start | bytes 1572868
  38.7 212.2 %collective-permute-start.8 = (bf16[1,3,4096]{2,1,0:T(4,128)(2,1)}, bf16[1,3,4096]{2,1,0:T(4,128)(2,1)}, u32[]{:S(2)}, u32[]{:S(2)}) collective-permute-start(bf16[1,3,4096]{2,1,0:T(4,128)(2,1)} %convert_bitcast_fusion.7), channel_id=1, source_target_pairs={{0,1},{1,2},{2,3},{3,4},{4,5},{5,6},{6,7},{7,8},{8,9},{9,10},{10,1... | collective-permute-start | bytes 73736 | tf_op jit(solution)/shard_map/ppermute | solution.py:20
  47.2 203.7 %collective-permute-start.9 = (bf16[1,3,4096]{2,1,0:T(4,128)(2,1)}, bf16[1,3,4096]{2,1,0:T(4,128)(2,1)}, u32[]{:S(2)}, u32[]{:S(2)}) collective-permute-start(bf16[1,3,4096]{2,1,0:T(4,128)(2,1)} %convert_bitcast_fusion.7), channel_id=1, source_target_pairs={{1,0},{2,1},{3,2},{4,3},{5,4},{6,5},{7,6},{8,7},{9,8},{10,9},{11,1... | collective-permute-start | bytes 73736 | tf_op jit(solution)/shard_map/ppermute | solution.py:21
  51.7 61.9 %copy-start.25 = (pred[32,512]{1,0:T(8,128)(4,1)}, pred[32,512]{1,0:T(8,128)(4,1)S(1)}, u32[]{:S(2)}) copy-start(pred[32,512]{1,0:T(8,128)(4,1)S(1)} %iota_compare_fusion.17) | copy-start | bytes 49156
  52.0 7.1 %collective-permute-start.1 = (bf16[3,512]{1,0:T(4,128)(2,1)S(1)}, bf16[3,512]{1,0:T(4,128)(2,1)S(1)}, u32[]{:S(2)}, u32[]{:S(2)}) collective-permute-start(bf16[3,512]{1,0:T(4,128)(2,1)S(1)} %select_convert_fusion.5), channel_id=1, source_target_pairs={{0,1},{1,2},{2,3},{3,4},{4,5},{5,6},{6,7},{7,8},{8,9},{9,10},{10,1... | collective-permute-start | bytes 9224 | tf_op jit(solution)/shard_map/ppermute | solution.py:29
  58.1 6.6 %collective-permute-start.3 = (bf16[3,512]{1,0:T(4,128)(2,1)S(1)}, bf16[3,512]{1,0:T(4,128)(2,1)S(1)}, u32[]{:S(2)}, u32[]{:S(2)}) collective-permute-start(bf16[3,512]{1,0:T(4,128)(2,1)S(1)} %select_convert_fusion.4), channel_id=1, source_target_pairs={{0,31},{1,0},{2,1},{3,2},{4,3},{5,4},{6,5},{7,6},{8,7},{9,8},{10,9... | collective-permute-start | bytes 9224 | tf_op jit(solution)/shard_map/ppermute | solution.py:29
  114.1 1.5 collective-permute-start.4
  114.2 6.9 %collective-permute-start.5 = (bf16[3,512]{1,0:T(4,128)(2,1)S(1)}, bf16[3,512]{1,0:T(4,128)(2,1)S(1)}, u32[]{:S(2)}, u32[]{:S(2)}) collective-permute-start(bf16[3,512]{1,0:T(4,128)(2,1)S(1)} %select_convert_fusion.2), channel_id=1, source_target_pairs={{0,31},{1,0},{2,1},{3,2},{4,3},{5,4},{6,5},{7,6},{8,7},{9,8},{10,9... | collective-permute-start | bytes 9224 | tf_op jit(solution)/shard_map/ppermute | solution.py:29
  183.2 1.3 collective-permute-start.6
  183.4 6.7 %collective-permute-start.7 = (bf16[3,512]{1,0:T(4,128)(2,1)S(1)}, bf16[3,512]{1,0:T(4,128)(2,1)S(1)}, u32[]{:S(2)}, u32[]{:S(2)}) collective-permute-start(bf16[3,512]{1,0:T(4,128)(2,1)S(1)} %select_convert_fusion), channel_id=1, source_target_pairs={{0,31},{1,0},{2,1},{3,2},{4,3},{5,4},{6,5},{7,6},{8,7},{9,8},{10,9... | collective-permute-start | bytes 9224 | tf_op jit(solution)/shard_map/ppermute | solution.py:29
  250.1 45.4 %copy-start.23 = (pred[32,4096]{1,0:T(8,128)(4,1)S(1)}, pred[32,4096]{1,0:T(8,128)(4,1)}, u32[]{:S(2)}) copy-start(pred[32,4096]{1,0:T(8,128)(4,1)} %iota_compare_fusion.13) | copy-start | bytes 393220
  250.1 45.4 %copy-start.30 = (s32[4096]{0:T(1024)S(1)}, s32[4096]{0:T(1024)}, u32[]{:S(2)}) copy-start(s32[4096]{0:T(1024)} %add_select_fusion.1) | copy-start | bytes 49156
  250.1 46.5 %copy-start.10 = (f32[3,4096]{1,0:T(4,128)S(1)}, f32[3,4096]{1,0:T(4,128)}, u32[]{:S(2)}) copy-start(f32[3,4096]{1,0:T(4,128)} %copy-done.8) | copy-start | bytes 147460
  250.1 46.5 %copy-start.12 = (f32[3,4096]{1,0:T(4,128)S(1)}, f32[3,4096]{1,0:T(4,128)}, u32[]{:S(2)}) copy-start(f32[3,4096]{1,0:T(4,128)} %copy-done.11) | copy-start | bytes 147460
  251.9 4.4 %collective-permute-start.10 = (bf16[1,3,4096]{2,1,0:T(4,128)(2,1)S(1)}, bf16[1,3,4096]{2,1,0:T(4,128)(2,1)S(1)}, u32[]{:S(2)}, u32[]{:S(2)}) collective-permute-start(bf16[1,3,4096]{2,1,0:T(4,128)(2,1)S(1)} %get-tuple-element.559), channel_id=1, source_target_pairs={{0,1},{1,2},{2,3},{3,4},{4,5},{5,6},{6,7},{7,8},{8,9},{9,10},{10,1... | collective-permute-start | bytes 73736 | tf_op jit(solution)/shard_map/ppermute | solution.py:20
  253.8 8.8 %collective-permute-start.11 = (bf16[1,3,4096]{2,1,0:T(4,128)(2,1)S(1)}, bf16[1,3,4096]{2,1,0:T(4,128)(2,1)S(1)}, u32[]{:S(2)}, u32[]{:S(2)}) collective-permute-start(bf16[1,3,4096]{2,1,0:T(4,128)(2,1)S(1)} %get-tuple-element.559), channel_id=1, source_target_pairs={{1,0},{2,1},{3,2},{4,3},{5,4},{6,5},{7,6},{8,7},{9,8},{10,9},{11,1... | collective-permute-start | bytes 73736 | tf_op jit(solution)/shard_map/ppermute | solution.py:21
  262.8 4.4 %collective-permute-start.12 = (bf16[1,3,4096]{2,1,0:T(4,128)(2,1)S(1)}, bf16[1,3,4096]{2,1,0:T(4,128)(2,1)S(1)}, u32[]{:S(2)}, u32[]{:S(2)}) collective-permute-start(bf16[1,3,4096]{2,1,0:T(4,128)(2,1)S(1)} %get-tuple-element.557), channel_id=1, source_target_pairs={{0,1},{1,2},{2,3},{3,4},{4,5},{5,6},{6,7},{7,8},{8,9},{9,10},{10,1... | collective-permute-start | bytes 73736 | tf_op jit(solution)/shard_map/ppermute | solution.py:20
  264.7 8.8 %collective-permute-start.13 = (bf16[1,3,4096]{2,1,0:T(4,128)(2,1)S(1)}, bf16[1,3,4096]{2,1,0:T(4,128)(2,1)S(1)}, u32[]{:S(2)}, u32[]{:S(2)}) collective-permute-start(bf16[1,3,4096]{2,1,0:T(4,128)(2,1)S(1)} %get-tuple-element.557), channel_id=1, source_target_pairs={{1,0},{2,1},{3,2},{4,3},{5,4},{6,5},{7,6},{8,7},{9,8},{10,9},{11,1... | collective-permute-start | bytes 73736 | tf_op jit(solution)/shard_map/ppermute | solution.py:21
  273.7 4.4 %collective-permute-start.14 = (bf16[1,3,4096]{2,1,0:T(4,128)(2,1)S(1)}, bf16[1,3,4096]{2,1,0:T(4,128)(2,1)S(1)}, u32[]{:S(2)}, u32[]{:S(2)}) collective-permute-start(bf16[1,3,4096]{2,1,0:T(4,128)(2,1)S(1)} %get-tuple-element.555), channel_id=1, source_target_pairs={{0,1},{1,2},{2,3},{3,4},{4,5},{5,6},{6,7},{7,8},{8,9},{9,10},{10,1... | collective-permute-start | bytes 73736 | tf_op jit(solution)/shard_map/ppermute | solution.py:20
  275.6 8.8 %collective-permute-start.15 = (bf16[1,3,4096]{2,1,0:T(4,128)(2,1)S(1)}, bf16[1,3,4096]{2,1,0:T(4,128)(2,1)S(1)}, u32[]{:S(2)}, u32[]{:S(2)}) collective-permute-start(bf16[1,3,4096]{2,1,0:T(4,128)(2,1)S(1)} %get-tuple-element.555), channel_id=1, source_target_pairs={{1,0},{2,1},{3,2},{4,3},{5,4},{6,5},{7,6},{8,7},{9,8},{10,9},{11,1... | collective-permute-start | bytes 73736 | tf_op jit(solution)/shard_map/ppermute | solution.py:21
  284.6 4.4 %collective-permute-start.16 = (bf16[1,3,4096]{2,1,0:T(4,128)(2,1)S(1)}, bf16[1,3,4096]{2,1,0:T(4,128)(2,1)S(1)}, u32[]{:S(2)}, u32[]{:S(2)}) collective-permute-start(bf16[1,3,4096]{2,1,0:T(4,128)(2,1)S(1)} %get-tuple-element.553), channel_id=1, source_target_pairs={{0,1},{1,2},{2,3},{3,4},{4,5},{5,6},{6,7},{7,8},{8,9},{9,10},{10,1... | collective-permute-start | bytes 73736 | tf_op jit(solution)/shard_map/ppermute | solution.py:20
  286.5 8.8 %collective-permute-start.17 = (bf16[1,3,4096]{2,1,0:T(4,128)(2,1)S(1)}, bf16[1,3,4096]{2,1,0:T(4,128)(2,1)S(1)}, u32[]{:S(2)}, u32[]{:S(2)}) collective-permute-start(bf16[1,3,4096]{2,1,0:T(4,128)(2,1)S(1)} %get-tuple-element.553), channel_id=1, source_target_pairs={{1,0},{2,1},{3,2},{4,3},{5,4},{6,5},{7,6},{8,7},{9,8},{10,9},{11,1... | collective-permute-start | bytes 73736 | tf_op jit(solution)/shard_map/ppermute | solution.py:21
  (37 other events, 156.3 us)
where the time goes:
time: 302 us; the launch traced here: 297 us
  other arithmetic  99.5 us (33%)
  matrix products  65.2 us (22%)
  waiting for transfers between devices  42.1 us (14%)
  starting transfers between devices  40 us (13%)
  blocking collectives  27.8 us (9%)
  local copies, waits for them, and re-layouts  19.2 us (6%)
    dot_general x55, matrix products, lookup_one_block(): jnp.dot(padded, onehot, preferred_element_type=jnp.float32, precision=pre...  63.7 us
    select_n x51, other arithmetic, lookup_one_block(): chosen = piece[None, :] // 128 == group_ids[:, None]  54.6 us
    psum x1, blocking collectives, body(): coarse_rhs = lax.psum(rhs_part, 'dom')  27.8 us
    ppermute x6, waiting for transfers between devices, with_halo(): after = lax.ppermute(initial, axis, down)  25.3 us
    reduce_sum x48, other arithmetic, lookup_one_block(): return jnp.sum(jnp.where(chosen[None, :, :], spread, 0.0), axis=1)  25.3 us
    ppermute x6, starting transfers between devices, with_halo(): before = lax.ppermute(last, axis, up)  20.9 us
    ppermute x6, waiting for transfers between devices, passed_along(): return lax.ppermute(value, axis, pairs)  16.7 us
    ppermute x6, starting transfers between devices, with_halo(): after = lax.ppermute(initial, axis, down)  12.2 us
  transfers between devices with their start and end apart: 18, of which 7 were waited for; matrix products, arithmetic and copies ran while one was open for 60% of the time, Pallas kernels for 0%

commit v1 on v0

--- a/solution.py
+++ b/solution.py
@@ -130,7 +130,11 @@
     per_group = coarse_dinv.shape[2]
     local_agg = aggregate - lax.axis_index("sub") * per_group
     rhs_part = accumulate(fine_residual, local_agg, per_group)
-    coarse_rhs = lax.psum(rhs_part, "dom")
+
+    def plane_take(base_x, peer_axis):
+        return jnp.sum(lax.all_gather(base_x, axis_name=peer_axis), 0)
+
+    coarse_rhs = plane_take(rhs_part, "dom")
     coarse_base = point_solve(coarse_dinv, coarse_rhs)
     coarse = coarse_base
     for iteration in range(JAC - 1):

time: 302 us -> 298 us (0.987)
    psum x1 -> x0, blocking collectives: 27.8 us -> none  [body(): coarse_rhs = lax.psum(rhs_part, 'dom')]
    all_gather x0 -> x1, blocking collectives: none -> 25.1 us  [plane_take(): return jnp.sum(lax.all_gather(base_x, axis_name=peer_axis), 0)]
  transfers between devices with their start and end apart: 18 -> 18, of which waited for: 7 -> 7; matrix products, arithmetic and copies ran while one was open for 60% -> 61% of each run, Pallas kernels for 0% -> 0%
where the time goes in v1:
time: 298 us; the launch traced here: 293 us
  other arithmetic  99.6 us (33%)
  matrix products  65.1 us (22%)
  waiting for transfers between devices  42.1 us (14%)
  starting transfers between devices  38.6 us (13%)
  blocking collectives  25.1 us (8%)
  local copies, waits for them, and re-layouts  19.2 us (6%)
    dot_general x55, matrix products, lookup_one_block(): jnp.dot(padded, onehot, preferred_element_type=jnp.float32, precision=pre...  63.6 us
    select_n x51, other arithmetic, lookup_one_block(): chosen = piece[None, :] // 128 == group_ids[:, None]  54.6 us
    ppermute x6, waiting for transfers between devices, with_halo(): after = lax.ppermute(initial, axis, down)  25.3 us
    reduce_sum x48, other arithmetic, lookup_one_block(): return jnp.sum(jnp.where(chosen[None, :, :], spread, 0.0), axis=1)  25.3 us
    all_gather x1, blocking collectives, plane_take(): return jnp.sum(lax.all_gather(base_x, axis_name=peer_axis), 0)  25.1 us
    ppermute x6, starting transfers between devices, with_halo(): before = lax.ppermute(last, axis, up)  19.4 us
    ppermute x6, waiting for transfers between devices, passed_along(): return lax.ppermute(value, axis, pairs)  16.7 us
    ppermute x6, starting transfers between devices, with_halo(): after = lax.ppermute(initial, axis, down)  12.2 us
  transfers between devices with their start and end apart: 18, of which 7 were waited for; matrix products, arithmetic and copies ran while one was open for 61% of the time, Pallas kernels for 0%

profile of v1, /device:TPU:101, one launch (start us, length us, event | category | flops | bytes accessed | tf_op | source)
XLA Modules:
  0.0 293.2 jit_solution(13204789894431686923)
XLA Ops:
  0.7 4.7 %collective-permute-start.2 = (s32[1,2,512]{2,1,0:T(2,128)}, s32[1,2,512]{2,1,0:T(2,128)S(1)}, u32[]{:S(2)}, u32[]{:S(2)}) collective-permute-start(s32[1,2,512]{2,1,0:T(2,128)} %param.19), channel_id=1, source_target_pairs={{0,1},{1,2},{2,3},{3,4},{4,5},{5,6},{6,7},{7,8},{8,9},{9,10},{10,1... | collective-permute-start | bytes 12296 | tf_op jit(solution)/shard_map/ppermute | solution.py:20
  6.7 3.5 %while.39 = (s32[]{:T(128)}, f32[96,128]{1,0:T(8,128)S(1)}, s32[2,2048]{1,0:T(2,128)S(1)}, f32[2,3,2048]{2,1,0:T(4,128)}, s32[]{:T(128)}, /*index=5*/s32[]{:T(128)}) while((s32[]{:T(128)}, f32[96,128]{1,0:T(8,128)S(1)}, s32[2,2048]{1,0:T(2,128)S(1)}, f32[2,3,2048]{2,1,0:T(4,128)}, s32[]{:T(128)}, /*index=5*/s32[]{:T(128)}) %tuple.160), condition=%wide.region_20.21_spmd.clone, body=%wide.region_19.20_spmd.clone.sunk | while | flops 302592000 | bytes 1933399 | solution.py:92
  10.2 25.1 %all_gather.3 = f32[8,3,4096]{2,1,0:T(4,128)S(1)} all-gather(f32[1,3,4096]{2,1,0:T(4,128)S(1)} %all_gather_reshape.3), channel_id=1, replica_groups=mesh['dom'=8,'sub'=32] {'dom'}, dimensions={0}, use_global_device_ids=true | all-gather | bytes 442368 | tf_op jit(solution)/shard_map/all_gather | solution.py:135
  36.1 7.1 %collective-permute-start.8 = (bf16[1,3,4096]{2,1,0:T(4,128)(2,1)}, bf16[1,3,4096]{2,1,0:T(4,128)(2,1)}, u32[]{:S(2)}, u32[]{:S(2)}) collective-permute-start(bf16[1,3,4096]{2,1,0:T(4,128)(2,1)} %convert_bitcast_fusion.7), channel_id=1, source_target_pairs={{0,1},{1,2},{2,3},{3,4},{4,5},{5,6},{6,7},{7,8},{8,9},{9,10},{10,1... | collective-permute-start | bytes 73736 | tf_op jit(solution)/shard_map/ppermute | solution.py:20
  43.2 1.9 collective-permute-start.9
  47.9 5.4 %collective-permute-start.1 = (bf16[3,512]{1,0:T(4,128)(2,1)S(1)}, bf16[3,512]{1,0:T(4,128)(2,1)S(1)}, u32[]{:S(2)}, u32[]{:S(2)}) collective-permute-start(bf16[3,512]{1,0:T(4,128)(2,1)S(1)} %select_convert_fusion.5), channel_id=1, source_target_pairs={{0,1},{1,2},{2,3},{3,4},{4,5},{5,6},{6,7},{7,8},{8,9},{9,10},{10,1... | collective-permute-start | bytes 9224 | tf_op jit(solution)/shard_map/ppermute | solution.py:29
  55.1 5.6 %collective-permute-done.3 = bf16[3,512]{1,0:T(4,128)(2,1)S(1)} collective-permute-done((bf16[3,512]{1,0:T(4,128)(2,1)S(1)}, bf16[3,512]{1,0:T(4,128)(2,1)S(1)}, u32[]{:S(2)}, u32[]{:S(2)}) %collective-permute-start.3) | collective-permute-done | bytes 3104 | tf_op jit(solution)/shard_map/ppermute | solution.py:29
  61.2 43.8 %while.36 = (s32[]{:T(128)}, bf16[16,3,8192]{2,1,0:T(4,128)(2,1)S(1)}, s32[16,8192]{1,0:T(8,128)}, bf16[120,128]{1,0:T(8,128)(2,1)S(1)}, s32[]{:T(128)}) while((s32[]{:T(128)}, bf16[16,3,8192]{2,1,0:T(4,128)(2,1)S(1)}, s32[16,8192]{1,0:T(8,128)}, bf16[120,128]{1,0:T(8,128)(2,1)S(1)}, s32[]{:T(128)}) %tuple.151), condition=%wide.region_5.6_spmd.clone, body=%wide.region_3.5_spmd.clone.sunk | while | flops 255139840 | bytes 8960069 | solution.py:63
  111.6 5.5 %collective-permute-done.5 = bf16[3,512]{1,0:T(4,128)(2,1)S(1)} collective-permute-done((bf16[3,512]{1,0:T(4,128)(2,1)S(1)}, bf16[3,512]{1,0:T(4,128)(2,1)S(1)}, u32[]{:S(2)}, u32[]{:S(2)}) %collective-permute-start.5) | collective-permute-done | bytes 3104 | tf_op jit(solution)/shard_map/ppermute | solution.py:29
  118.2 55.8 %while.37 = (s32[]{:T(128)}, bf16[16,3,8192]{2,1,0:T(4,128)(2,1)S(1)}, s32[16,8192]{1,0:T(8,128)}, bf16[120,128]{1,0:T(8,128)(2,1)}, s32[]{:T(128)}) while((s32[]{:T(128)}, bf16[16,3,8192]{2,1,0:T(4,128)(2,1)S(1)}, s32[16,8192]{1,0:T(8,128)}, bf16[120,128]{1,0:T(8,128)(2,1)}, s32[]{:T(128)}) %tuple.154), condition=%wide.region_11.12_spmd.clone, body=%wide.region_9.11_spmd.clone.sunk | while | flops 255139840 | bytes 8960069 | solution.py:63
  180.4 5.6 %collective-permute-done.7 = bf16[3,512]{1,0:T(4,128)(2,1)S(1)} collective-permute-done((bf16[3,512]{1,0:T(4,128)(2,1)S(1)}, bf16[3,512]{1,0:T(4,128)(2,1)S(1)}, u32[]{:S(2)}, u32[]{:S(2)}) %collective-permute-start.7) | collective-permute-done | bytes 3104 | tf_op jit(solution)/shard_map/ppermute | solution.py:29
  187.0 55.8 %while.38 = (s32[]{:T(128)}, bf16[16,3,8192]{2,1,0:T(4,128)(2,1)S(1)}, s32[16,8192]{1,0:T(8,128)}, bf16[120,128]{1,0:T(8,128)(2,1)}, s32[]{:T(128)}) while((s32[]{:T(128)}, bf16[16,3,8192]{2,1,0:T(4,128)(2,1)S(1)}, s32[16,8192]{1,0:T(8,128)}, bf16[120,128]{1,0:T(8,128)(2,1)}, s32[]{:T(128)}) %tuple.157), condition=%wide.region_17.18_spmd.clone, body=%wide.region_15.17_spmd.clone.sunk | while | flops 255139840 | bytes 8960069 | solution.py:63
  247.7 1.9 collective-permute-start.10
  249.7 2.4 collective-permute-start.11
  252.2 6.3 %collective-permute-done.11 = bf16[1,3,4096]{2,1,0:T(4,128)(2,1)S(1)} collective-permute-done((bf16[1,3,4096]{2,1,0:T(4,128)(2,1)S(1)}, bf16[1,3,4096]{2,1,0:T(4,128)(2,1)S(1)}, u32[]{:S(2)}, u32[]{:S(2)}) %collective-permute-start.11) | collective-permute-done | bytes 24608 | tf_op jit(solution)/shard_map/ppermute | solution.py:21
  258.6 1.9 collective-permute-start.12
  260.6 2.4 collective-permute-start.13
  263.1 6.3 %collective-permute-done.13 = bf16[1,3,4096]{2,1,0:T(4,128)(2,1)S(1)} collective-permute-done((bf16[1,3,4096]{2,1,0:T(4,128)(2,1)S(1)}, bf16[1,3,4096]{2,1,0:T(4,128)(2,1)S(1)}, u32[]{:S(2)}, u32[]{:S(2)}) %collective-permute-start.13) | collective-permute-done | bytes 24608 | tf_op jit(solution)/shard_map/ppermute | solution.py:21
  269.5 1.9 collective-permute-start.14
  271.5 2.4 collective-permute-start.15
  274.0 6.3 %collective-permute-done.15 = bf16[1,3,4096]{2,1,0:T(4,128)(2,1)S(1)} collective-permute-done((bf16[1,3,4096]{2,1,0:T(4,128)(2,1)S(1)}, bf16[1,3,4096]{2,1,0:T(4,128)(2,1)S(1)}, u32[]{:S(2)}, u32[]{:S(2)}) %collective-permute-start.15) | collective-permute-done | bytes 24608 | tf_op jit(solution)/shard_map/ppermute | solution.py:21
  280.4 1.9 collective-permute-start.16
  282.4 2.4 collective-permute-start.17
  284.9 6.3 %collective-permute-done.17 = bf16[1,3,4096]{2,1,0:T(4,128)(2,1)S(1)} collective-permute-done((bf16[1,3,4096]{2,1,0:T(4,128)(2,1)S(1)}, bf16[1,3,4096]{2,1,0:T(4,128)(2,1)S(1)}, u32[]{:S(2)}, u32[]{:S(2)}) %collective-permute-start.17) | collective-permute-done | bytes 24608 | tf_op jit(solution)/shard_map/ppermute | solution.py:21
  (478 shorter events, 186.1 us)
Async XLA Ops:
  0.0 47.6 %collective-permute-start = (s32[1,2,512]{2,1,0:T(2,128)}, s32[1,2,512]{2,1,0:T(2,128)S(1)}, u32[]{:S(2)}, u32[]{:S(2)}) collective-permute-start(s32[1,2,512]{2,1,0:T(2,128)} %param.19), channel_id=1, source_target_pairs={{1,0},{2,1},{3,2},{4,3},{5,4},{6,5},{7,6},{8,7},{9,8},{10,9},{11,1... | collective-permute-start | bytes 12296 | tf_op jit(solution)/shard_map/ppermute | solution.py:21
  0.7 52.7 %collective-permute-start.2 = (s32[1,2,512]{2,1,0:T(2,128)}, s32[1,2,512]{2,1,0:T(2,128)S(1)}, u32[]{:S(2)}, u32[]{:S(2)}) collective-permute-start(s32[1,2,512]{2,1,0:T(2,128)} %param.19), channel_id=1, source_target_pairs={{0,1},{1,2},{2,3},{3,4},{4,5},{5,6},{6,7},{7,8},{8,9},{9,10},{10,1... | collective-permute-start | bytes 12296 | tf_op jit(solution)/shard_map/ppermute | solution.py:20
  6.1 47.9 %copy-start.17 = (s32[32,4096]{1,0:T(8,128)S(1)}, s32[32,4096]{1,0:T(8,128)}, u32[]{:S(2)}) copy-start(s32[32,4096]{1,0:T(8,128)} %param.18) | copy-start | bytes 1572868
  36.1 210.7 %collective-permute-start.8 = (bf16[1,3,4096]{2,1,0:T(4,128)(2,1)}, bf16[1,3,4096]{2,1,0:T(4,128)(2,1)}, u32[]{:S(2)}, u32[]{:S(2)}) collective-permute-start(bf16[1,3,4096]{2,1,0:T(4,128)(2,1)} %convert_bitcast_fusion.7), channel_id=1, source_target_pairs={{0,1},{1,2},{2,3},{3,4},{4,5},{5,6},{6,7},{7,8},{8,9},{9,10},{10,1... | collective-permute-start | bytes 73736 | tf_op jit(solution)/shard_map/ppermute | solution.py:20
  43.2 203.6 %collective-permute-start.9 = (bf16[1,3,4096]{2,1,0:T(4,128)(2,1)}, bf16[1,3,4096]{2,1,0:T(4,128)(2,1)}, u32[]{:S(2)}, u32[]{:S(2)}) collective-permute-start(bf16[1,3,4096]{2,1,0:T(4,128)(2,1)} %convert_bitcast_fusion.7), channel_id=1, source_target_pairs={{1,0},{2,1},{3,2},{4,3},{5,4},{6,5},{7,6},{8,7},{9,8},{10,9},{11,1... | collective-permute-start | bytes 73736 | tf_op jit(solution)/shard_map/ppermute | solution.py:21
  47.7 61.9 %copy-start.25 = (pred[32,512]{1,0:T(8,128)(4,1)}, pred[32,512]{1,0:T(8,128)(4,1)S(1)}, u32[]{:S(2)}) copy-start(pred[32,512]{1,0:T(8,128)(4,1)S(1)} %iota_compare_fusion.17) | copy-start | bytes 49156
  47.9 7.1 %collective-permute-start.1 = (bf16[3,512]{1,0:T(4,128)(2,1)S(1)}, bf16[3,512]{1,0:T(4,128)(2,1)S(1)}, u32[]{:S(2)}, u32[]{:S(2)}) collective-permute-start(bf16[3,512]{1,0:T(4,128)(2,1)S(1)} %select_convert_fusion.5), channel_id=1, source_target_pairs={{0,1},{1,2},{2,3},{3,4},{4,5},{5,6},{6,7},{7,8},{8,9},{9,10},{10,1... | collective-permute-start | bytes 9224 | tf_op jit(solution)/shard_map/ppermute | solution.py:29
  54.0 6.6 %collective-permute-start.3 = (bf16[3,512]{1,0:T(4,128)(2,1)S(1)}, bf16[3,512]{1,0:T(4,128)(2,1)S(1)}, u32[]{:S(2)}, u32[]{:S(2)}) collective-permute-start(bf16[3,512]{1,0:T(4,128)(2,1)S(1)} %select_convert_fusion.4), channel_id=1, source_target_pairs={{0,31},{1,0},{2,1},{3,2},{4,3},{5,4},{6,5},{7,6},{8,7},{9,8},{10,9... | collective-permute-start | bytes 9224 | tf_op jit(solution)/shard_map/ppermute | solution.py:29
  110.0 1.5 collective-permute-start.4
  110.2 6.9 %collective-permute-start.5 = (bf16[3,512]{1,0:T(4,128)(2,1)S(1)}, bf16[3,512]{1,0:T(4,128)(2,1)S(1)}, u32[]{:S(2)}, u32[]{:S(2)}) collective-permute-start(bf16[3,512]{1,0:T(4,128)(2,1)S(1)} %select_convert_fusion.2), channel_id=1, source_target_pairs={{0,31},{1,0},{2,1},{3,2},{4,3},{5,4},{6,5},{7,6},{8,7},{9,8},{10,9... | collective-permute-start | bytes 9224 | tf_op jit(solution)/shard_map/ppermute | solution.py:29
  179.1 1.3 collective-permute-start.6
  179.2 6.7 %collective-permute-start.7 = (bf16[3,512]{1,0:T(4,128)(2,1)S(1)}, bf16[3,512]{1,0:T(4,128)(2,1)S(1)}, u32[]{:S(2)}, u32[]{:S(2)}) collective-permute-start(bf16[3,512]{1,0:T(4,128)(2,1)S(1)} %select_convert_fusion), channel_id=1, source_target_pairs={{0,31},{1,0},{2,1},{3,2},{4,3},{5,4},{6,5},{7,6},{8,7},{9,8},{10,9... | collective-permute-start | bytes 9224 | tf_op jit(solution)/shard_map/ppermute | solution.py:29
  245.9 45.4 %copy-start.23 = (pred[32,4096]{1,0:T(8,128)(4,1)S(1)}, pred[32,4096]{1,0:T(8,128)(4,1)}, u32[]{:S(2)}) copy-start(pred[32,4096]{1,0:T(8,128)(4,1)} %iota_compare_fusion.13) | copy-start | bytes 393220
  245.9 45.4 %copy-start.30 = (s32[4096]{0:T(1024)S(1)}, s32[4096]{0:T(1024)}, u32[]{:S(2)}) copy-start(s32[4096]{0:T(1024)} %add_select_fusion.1) | copy-start | bytes 49156
  246.0 46.5 %copy-start.10 = (f32[3,4096]{1,0:T(4,128)S(1)}, f32[3,4096]{1,0:T(4,128)}, u32[]{:S(2)}) copy-start(f32[3,4096]{1,0:T(4,128)} %copy-done.8) | copy-start | bytes 147460
  246.0 46.5 %copy-start.12 = (f32[3,4096]{1,0:T(4,128)S(1)}, f32[3,4096]{1,0:T(4,128)}, u32[]{:S(2)}) copy-start(f32[3,4096]{1,0:T(4,128)} %copy-done.11) | copy-start | bytes 147460
  247.7 4.4 %collective-permute-start.10 = (bf16[1,3,4096]{2,1,0:T(4,128)(2,1)S(1)}, bf16[1,3,4096]{2,1,0:T(4,128)(2,1)S(1)}, u32[]{:S(2)}, u32[]{:S(2)}) collective-permute-start(bf16[1,3,4096]{2,1,0:T(4,128)(2,1)S(1)} %get-tuple-element.559), channel_id=1, source_target_pairs={{0,1},{1,2},{2,3},{3,4},{4,5},{5,6},{6,7},{7,8},{8,9},{9,10},{10,1... | collective-permute-start | bytes 73736 | tf_op jit(solution)/shard_map/ppermute | solution.py:20
  249.7 8.8 %collective-permute-start.11 = (bf16[1,3,4096]{2,1,0:T(4,128)(2,1)S(1)}, bf16[1,3,4096]{2,1,0:T(4,128)(2,1)S(1)}, u32[]{:S(2)}, u32[]{:S(2)}) collective-permute-start(bf16[1,3,4096]{2,1,0:T(4,128)(2,1)S(1)} %get-tuple-element.559), channel_id=1, source_target_pairs={{1,0},{2,1},{3,2},{4,3},{5,4},{6,5},{7,6},{8,7},{9,8},{10,9},{11,1... | collective-permute-start | bytes 73736 | tf_op jit(solution)/shard_map/ppermute | solution.py:21
  258.6 4.4 %collective-permute-start.12 = (bf16[1,3,4096]{2,1,0:T(4,128)(2,1)S(1)}, bf16[1,3,4096]{2,1,0:T(4,128)(2,1)S(1)}, u32[]{:S(2)}, u32[]{:S(2)}) collective-permute-start(bf16[1,3,4096]{2,1,0:T(4,128)(2,1)S(1)} %get-tuple-element.557), channel_id=1, source_target_pairs={{0,1},{1,2},{2,3},{3,4},{4,5},{5,6},{6,7},{7,8},{8,9},{9,10},{10,1... | collective-permute-start | bytes 73736 | tf_op jit(solution)/shard_map/ppermute | solution.py:20
  260.6 8.8 %collective-permute-start.13 = (bf16[1,3,4096]{2,1,0:T(4,128)(2,1)S(1)}, bf16[1,3,4096]{2,1,0:T(4,128)(2,1)S(1)}, u32[]{:S(2)}, u32[]{:S(2)}) collective-permute-start(bf16[1,3,4096]{2,1,0:T(4,128)(2,1)S(1)} %get-tuple-element.557), channel_id=1, source_target_pairs={{1,0},{2,1},{3,2},{4,3},{5,4},{6,5},{7,6},{8,7},{9,8},{10,9},{11,1... | collective-permute-start | bytes 73736 | tf_op jit(solution)/shard_map/ppermute | solution.py:21
  269.5 4.4 %collective-permute-start.14 = (bf16[1,3,4096]{2,1,0:T(4,128)(2,1)S(1)}, bf16[1,3,4096]{2,1,0:T(4,128)(2,1)S(1)}, u32[]{:S(2)}, u32[]{:S(2)}) collective-permute-start(bf16[1,3,4096]{2,1,0:T(4,128)(2,1)S(1)} %get-tuple-element.555), channel_id=1, source_target_pairs={{0,1},{1,2},{2,3},{3,4},{4,5},{5,6},{6,7},{7,8},{8,9},{9,10},{10,1... | collective-permute-start | bytes 73736 | tf_op jit(solution)/shard_map/ppermute | solution.py:20
  271.5 8.8 %collective-permute-start.15 = (bf16[1,3,4096]{2,1,0:T(4,128)(2,1)S(1)}, bf16[1,3,4096]{2,1,0:T(4,128)(2,1)S(1)}, u32[]{:S(2)}, u32[]{:S(2)}) collective-permute-start(bf16[1,3,4096]{2,1,0:T(4,128)(2,1)S(1)} %get-tuple-element.555), channel_id=1, source_target_pairs={{1,0},{2,1},{3,2},{4,3},{5,4},{6,5},{7,6},{8,7},{9,8},{10,9},{11,1... | collective-permute-start | bytes 73736 | tf_op jit(solution)/shard_map/ppermute | solution.py:21
  280.4 4.4 %collective-permute-start.16 = (bf16[1,3,4096]{2,1,0:T(4,128)(2,1)S(1)}, bf16[1,3,4096]{2,1,0:T(4,128)(2,1)S(1)}, u32[]{:S(2)}, u32[]{:S(2)}) collective-permute-start(bf16[1,3,4096]{2,1,0:T(4,128)(2,1)S(1)} %get-tuple-element.553), channel_id=1, source_target_pairs={{0,1},{1,2},{2,3},{3,4},{4,5},{5,6},{6,7},{7,8},{8,9},{9,10},{10,1... | collective-permute-start | bytes 73736 | tf_op jit(solution)/shard_map/ppermute | solution.py:20
  282.4 8.8 %collective-permute-start.17 = (bf16[1,3,4096]{2,1,0:T(4,128)(2,1)S(1)}, bf16[1,3,4096]{2,1,0:T(4,128)(2,1)S(1)}, u32[]{:S(2)}, u32[]{:S(2)}) collective-permute-start(bf16[1,3,4096]{2,1,0:T(4,128)(2,1)S(1)} %get-tuple-element.553), channel_id=1, source_target_pairs={{1,0},{2,1},{3,2},{4,3},{5,4},{6,5},{7,6},{8,7},{9,8},{10,9},{11,1... | collective-permute-start | bytes 73736 | tf_op jit(solution)/shard_map/ppermute | solution.py:21
  (37 other events, 149.7 us)
